TPU v7x, 512 devices: a whole 4x4x16 slice. The times are simulated.
512 devices in a mesh: tr: 64 (over x, z), ct: 8 (over y, core).
Axes of the slice: x: 4, y: 4, z: 16, core: 2. Of those that a mesh axis runs over, the one named last changes fastest.
Arguments:
- amplitudes: bfloat16 [8, 4096, 2, 4096], P(None, 'tr', None, 'ct'), may hold values from -6 to 6
- cycle_integrals: bfloat16 [2, 4096, 1, 4096], P(None, 'ct', None, 'tr'), may hold values from -0.0625 to 0.0625
- pair_live: int32 [8, 64], replicated, may hold values 0 or 1
Outputs:
- permuted: bfloat16 [8, 4096, 1, 4096], P('ct', 'tr')
All inputs are finite; a program needn't handle non-finite values.
Results may differ from a plain program's by a relative error of at most 0.017.
Values may be sent and summed in bfloat16 or wider, within the bound.
A program may use at most 64 MiB of HBM per device.

v0:
```python
import jax
import jax.numpy as jnp
from jax import lax
from jax.sharding import PartitionSpec as P


def per_device(amplitudes, cycle_integrals, pair_live):
    tile_size = amplitudes.shape[1]
    block_cols = amplitudes.shape[3]
    occ_k = amplitudes.shape[2]
    row_index = lax.axis_index("tr")
    col_index = lax.axis_index("ct")
    row_live = lax.dynamic_slice_in_dim(pair_live, row_index, 1, 1).astype(jnp.bfloat16)
    col_full = jnp.repeat(pair_live[:occ_k], tile_size, axis=1)
    col_live = lax.dynamic_slice_in_dim(col_full, col_index * block_cols, block_cols, 1).astype(
        jnp.bfloat16
    )
    masked = amplitudes * row_live[:, :, None, None] * col_live[None, None, :, :]
    partial_value = jnp.einsum(
        "iakc,kcjb->iajb",
        masked,
        lax.all_gather(cycle_integrals, "tr", axis=3, tiled=True),
        preferred_element_type=jnp.float32,
    )
    moved_parts = lax.all_to_all(
        partial_value.astype(jnp.bfloat16), "tr", split_axis=3, concat_axis=1, tiled=True
    )
    moved = lax.psum_scatter(
        moved_parts.astype(jnp.float32).astype(jnp.bfloat16), "ct", scatter_dimension=0, tiled=True
    )
    return jnp.transpose(moved, (0, 3, 2, 1))


def solution(mesh):
    return jax.shard_map(
        per_device,
        mesh=mesh,
        in_specs=(P(None, "tr", None, "ct"), P(None, "ct", None, "tr"), P()),
        out_specs=P("ct", "tr", None, None),
        check_vma=False,
    )
```

profile of v0, /device:TPU:2, one launch (start us, length us, event | category | flops | bytes accessed | tf_op | source)
XLA Modules:
  0.0 500.7 jit_solution(14204285625697679978)
XLA Ops:
  6.5 0.0 all-gather.2.cloned.1.call-start
  6.5 1.7 copy.7
  8.2 0.0 all-gather.2.cloned.1.call-update
  8.3 0.0 reduce-scatter.2.cloned.1.call-start
  8.3 0.7 slice.3
  9.0 0.9 fusion.8
  9.9 0.1 broadcast_in_dim.2
  9.9 0.1 reshape.10
  10.1 2.3 multiply_multiply_fusion
  12.4 158.5 %all-gather.2.cloned.1.call-done = bf16[2,512,1,4096]{1,0,2,3:T(2,128)(2,1)} async-done(((bf16[2,512,1,64]{1,0,2,3:T(2,128)(2,1)}), bf16[2,512,1,4096]{1,0,2,3:T(2,128)(2,1)}) %all-gather.2.cloned.1.call-update) | async-done | bytes 8388624 | tf_op jit(solution)/shard_map/all_gather | solution.py:22
  170.8 21.3 %copy.8 = bf16[2,512,1,4096]{3,1,0,2:T(8,128)(2,1)} copy(bf16[2,512,1,4096]{1,0,2,3:T(2,128)(2,1)} %all-gather.2.cloned.1.call-done) | data formatting | bytes 16777216 | tf_op jit(solution)/shard_map/all_gather | solution.py:22
  192.1 9.4 %fusion.4 = bf16[8,64,1,4096]{3,1,0,2:T(8,128)(2,1)} fusion(bf16[2,512,1,4096]{3,1,0,2:T(8,128)(2,1)} %copy.8, bf16[8,64,2,512]{3,2,1,0:T(2,128)(2,1)S(1)} %multiply_multiply_fusion), kind=kOutput, calls=%fused_computation.3 | convolution fusion | flops 4297064448 | bytes 13631488 | tf_op jit(solution)/shard_map/iakc,kcjb->iajb/dot_general | solution.py:19
  201.5 10.0 %copy.10 = bf16[8,64,1,4096]{1,0,2,3:T(8,128)(2,1)} copy(bf16[8,64,1,4096]{3,1,0,2:T(8,128)(2,1)} %fusion.4) | data formatting | bytes 8388608 | tf_op jit(solution)/shard_map/convert_element_type | solution.py:26
  211.5 14.3 %reshape.15 = bf16[64,2,16384]{2,1,0:T(2,128)(2,1)} reshape(bf16[4096,1,8,64]{3,2,1,0:T(8,128)(2,1)} %bitcast.25) | data formatting | bytes 8388608
  225.8 187.9 %all_to_all.18 = bf16[64,2,16384]{2,1,0:T(2,128)(2,1)} all-to-all(bf16[64,2,16384]{2,1,0:T(2,128)(2,1)} %reshape.15), channel_id=1, replica_groups=mesh['tr'=64,'ct'=8] {'tr'}, dimensions={0} | all-to-all | bytes 8388608 | tf_op jit(solution)/shard_map/all_to_all | solution.py:25
  413.8 14.6 %reshape.16 = bf16[4096,1,8,64]{3,2,1,0:T(8,128)(2,1)} reshape(bf16[64,2,16384]{2,1,0:T(2,128)(2,1)} %all_to_all.18) | data formatting | bytes 8388608
  428.4 12.0 %copy.11 = bf16[8,64,64,1,64]{2,1,4,0,3:T(8,128)(2,1)} copy(bf16[8,64,64,1,64]{2,0,4,1,3:T(8,128)(2,1)} %bitcast.26) | data formatting | bytes 8388608 | tf_op jit(solution)/shard_map/all_to_all | solution.py:25
  440.4 12.1 %all_to_all.16 = bf16[8,4096,1,64]{1,3,2,0:T(8,128)(2,1)} reshape(bf16[8,64,64,1,64]{2,1,4,0,3:T(8,128)(2,1)} %copy.11) | data formatting | bytes 8388608 | tf_op jit(solution)/shard_map/all_to_all | solution.py:25
  452.4 0.0 reduce-scatter.2.cloned.1.call-update
  452.4 41.4 %reduce-scatter.2.cloned.1.call-done = bf16[1,4096,1,64]{1,3,2,0:T(8,128)(2,1)} async-done(((bf16[8,4096,1,64]{1,3,2,0:T(8,128)(2,1)}), bf16[1,4096,1,64]{1,3,2,0:T(8,128)(2,1)}) %reduce-scatter.2.cloned.1.call-update) | async-done | bytes 524304 | tf_op jit(solution)/shard_map/reduce_scatter | solution.py:28
  (1 shorter events, 0.0 us)
Async XLA Ops:
  6.5 164.3 %all-gather.2.cloned.1.call-start = ((), (), s32[]{:S(2)}) async-start(), calls=%async_computation.2 | async-start | bytes 8519680 | tf_op jit(solution)/shard_map/all_gather | solution.py:22
  8.3 485.6 %reduce-scatter.2.cloned.1.call-start = ((), (), s32[]{:S(2)}) async-start(), calls=%async_computation.3 | async-start | bytes 4718592 | tf_op jit(solution)/shard_map/reduce_scatter | solution.py:28
Sparse Core Ops, SparseCore 0:
  10.3 160.4 all-gather.1
  452.6 41.2 reduce-scatter.1
where the time goes:
time: 503 us; the launch traced here: 501 us
  waiting for transfers between devices  200 us (40%)
  blocking collectives  188 us (37%)
  local copies, waits for them, and re-layouts  86.8 us (17%)
  between operations  13.4 us (3%)
  matrix products  9.39 us (2%)
    all_to_all x1, blocking collectives, per_device(): lax.all_to_all(partial_value.astype(jnp.bfloat16), 'tr', split_axis=3, co...  188 us
    all_gather x1, waiting for transfers between devices, per_device(): lax.all_gather(cycle_integrals, 'tr', axis=3, tiled=True)  158 us
    reduce_scatter x1, waiting for transfers between devices, per_device(): lax.psum_scatter(moved_parts.astype(jnp.float32).astype(jnp.bfloat16), 'c...  41.4 us
    unnamed x3, local copies, waits for them, and re-layouts  30.6 us
    all_to_all x2, local copies, waits for them, and re-layouts, per_device(): lax.all_to_all(partial_value.astype(jnp.bfloat16), 'tr', split_axis=3, co...  24 us
    all_gather x1, local copies, waits for them, and re-layouts, per_device(): lax.all_gather(cycle_integrals, 'tr', axis=3, tiled=True)  21.3 us
  transfers between devices with their start and end apart: 2, of which 2 were waited for; matrix products, arithmetic and copies ran while one was open for 1% of the time, Pallas kernels for 0%

commit v1 on v0

--- a/solution.py
+++ b/solution.py
@@ -19,7 +19,9 @@
     partial_value = jnp.einsum(
         "iakc,kcjb->iajb",
         masked,
-        lax.all_gather(cycle_integrals, "tr", axis=3, tiled=True),
+        jnp.concatenate(
+            lax.all_to_all(jnp.stack([cycle_integrals] * lax.axis_size("tr")), "tr", 0, 0), axis=3
+        ),
         preferred_element_type=jnp.float32,
     )
     moved_parts = lax.all_to_all(

time: 503 us -> 721 us (1.43)
  the two profiles are of different devices: /device:TPU:2 before, /device:TPU:6 now
where the time goes in v1:
time: 721 us; the launch traced here: 719 us
  waiting for transfers between devices  403 us (56%)
  blocking collectives  197 us (27%)
  local copies, waits for them, and re-layouts  76.1 us (11%)
  starting transfers between devices  19.2 us (3%)
  between operations  13.5 us (2%)
  matrix products  9.52 us (1%)
    all_to_all x1, waiting for transfers between devices, per_device(): lax.all_to_all(jnp.stack([cycle_integrals] * lax.axis_size('tr')), 'tr',...  364 us
    all_to_all x1, blocking collectives, per_device(): lax.all_to_all(partial_value.astype(jnp.bfloat16), 'tr', split_axis=3, co...  197 us
    reduce_scatter x1, waiting for transfers between devices, per_device(): lax.psum_scatter(moved_parts.astype(jnp.float32).astype(jnp.bfloat16), 'c...  38.8 us
    unnamed x6, local copies, waits for them, and re-layouts  28.9 us
    all_to_all x2, local copies, waits for them, and re-layouts, per_device(): lax.all_to_all(partial_value.astype(jnp.bfloat16), 'tr', split_axis=3, co...  24 us
    all_to_all x1, starting transfers between devices, per_device(): lax.all_to_all(jnp.stack([cycle_integrals] * lax.axis_size('tr')), 'tr',...  19.1 us
  transfers between devices with their start and end apart: 2, of which 2 were waited for; matrix products, arithmetic and copies ran while one was open for 0% of the time, Pallas kernels for 0%

profile of v1, /device:TPU:6, one launch (start us, length us, event | category | flops | bytes accessed | tf_op | source)
XLA Modules:
  0.0 719.5 jit_solution(9117766954884938592)
XLA Ops:
  6.5 5.2 stack.2
  11.7 0.0 copy-start.1
  11.7 0.0 slice-start
  11.7 0.0 copy-start
  11.7 19.1 %all-to-all-start = ((bf16[64,2,512,1,64]{2,4,1,3,0:T(8,128)(2,1)}), bf16[64,2,512,1,64]{2,4,1,3,0:T(8,128)(2,1)}, u32[]{:S(2)}, u32[]{:S(2)}) async-start(bf16[64,2,512,1,64]{2,4,1,3,0:T(8,128)(2,1)} %stack.2), calls=%async_computation | async-start | bytes 16777216 | tf_op jit(solution)/shard_map/all_to_all | solution.py:23
  30.8 0.0 reduce-scatter.2.cloned.1.call-start
  30.9 0.0 copy-done.1
  30.9 0.2 fusion.2
  31.1 0.0 slice-done
  31.1 0.1 broadcast_in_dim.2
  31.2 0.1 reshape.18
  31.3 0.0 copy-done
  31.3 1.1 multiply_multiply_fusion
  32.4 363.9 %all-to-all-done = bf16[64,2,512,1,64]{2,4,1,3,0:T(8,128)(2,1)} async-done(((bf16[64,2,512,1,64]{2,4,1,3,0:T(8,128)(2,1)}), bf16[64,2,512,1,64]{2,4,1,3,0:T(8,128)(2,1)}, u32[]{:S(2)}, u32[]{:S(2)}) %all-to-all-start) | async-done | bytes 8388640 | tf_op jit(solution)/shard_map/all_to_all | solution.py:23
  396.3 7.7 %copy.10 = bf16[64,2,512,1,64]{2,4,0,1,3:T(8,128)(2,1)} copy(bf16[64,2,512,1,64]{2,4,1,3,0:T(8,128)(2,1)} %all-to-all-done) | data formatting | bytes 16777216 | tf_op jit(solution)/shard_map/all_to_all | solution.py:23
  404.0 9.5 %fusion = bf16[8,64,1,4096]{3,1,0,2:T(8,128)(2,1)} fusion(bf16[2,512,4096,1]{1,2,0,3:T(8,128)(2,1)} %bitcast.26, bf16[8,64,2,512]{3,2,1,0:T(2,128)(2,1)S(1)} %multiply_multiply_fusion), kind=kOutput, calls=%fused_computation.1 | convolution fusion | flops 4297064448 | bytes 13631488 | tf_op jit(solution)/shard_map/iakc,kcjb->iajb/dot_general | solution.py:19
  413.5 10.0 %copy.13 = bf16[8,64,1,4096]{1,0,2,3:T(8,128)(2,1)} copy(bf16[8,64,1,4096]{3,1,0,2:T(8,128)(2,1)} %fusion) | data formatting | bytes 8388608 | tf_op jit(solution)/shard_map/convert_element_type | solution.py:28
  423.6 14.3 %reshape.24 = bf16[64,2,16384]{2,1,0:T(2,128)(2,1)} reshape(bf16[4096,1,8,64]{3,2,1,0:T(8,128)(2,1)} %bitcast.24) | data formatting | bytes 8388608
  437.9 197.3 %all_to_all.23 = bf16[64,2,16384]{2,1,0:T(2,128)(2,1)} all-to-all(bf16[64,2,16384]{2,1,0:T(2,128)(2,1)} %reshape.24), channel_id=1, replica_groups=mesh['tr'=64,'ct'=8] {'tr'}, dimensions={0} | all-to-all | bytes 8388608 | tf_op jit(solution)/shard_map/all_to_all | solution.py:27
  635.1 14.6 %reshape.25 = bf16[4096,1,8,64]{3,2,1,0:T(8,128)(2,1)} reshape(bf16[64,2,16384]{2,1,0:T(2,128)(2,1)} %all_to_all.23) | data formatting | bytes 8388608
  649.7 12.0 %copy.14 = bf16[8,64,64,1,64]{2,1,4,0,3:T(8,128)(2,1)} copy(bf16[8,64,64,1,64]{2,0,4,1,3:T(8,128)(2,1)} %bitcast.25) | data formatting | bytes 8388608 | tf_op jit(solution)/shard_map/all_to_all | solution.py:27
  661.7 12.0 %all_to_all.20 = bf16[8,4096,1,64]{1,3,2,0:T(8,128)(2,1)} reshape(bf16[8,64,64,1,64]{2,1,4,0,3:T(8,128)(2,1)} %copy.14) | data formatting | bytes 8388608 | tf_op jit(solution)/shard_map/all_to_all | solution.py:27
  673.8 0.0 reduce-scatter.2.cloned.1.call-update
  673.8 38.8 %reduce-scatter.2.cloned.1.call-done = bf16[1,4096,1,64]{1,3,2,0:T(8,128)(2,1)} async-done(((bf16[8,4096,1,64]{1,3,2,0:T(8,128)(2,1)}), bf16[1,4096,1,64]{1,3,2,0:T(8,128)(2,1)}) %reduce-scatter.2.cloned.1.call-update) | async-done | bytes 524304 | tf_op jit(solution)/shard_map/reduce_scatter | solution.py:30
  (1 shorter events, 0.0 us)
Async XLA Ops:
  11.7 19.2 %copy-start.1 = (s32[8,64]{1,0:T(8,128)S(1)}, s32[8,64]{1,0:T(8,128)}, u32[]{:S(2)}) copy-start(s32[8,64]{1,0:T(8,128)} %param.5) | copy-start | bytes 6148
  11.7 19.4 %slice-start = ((s32[8,64]{1,0:T(8,128)}), s32[2,64]{1,0:T(2,128)S(1)}, s32[]{:S(2)}) async-start(s32[8,64]{1,0:T(8,128)} %param.5), calls=%async_computation.4 | async-start | bytes 2048 | tf_op jit(solution)/shard_map/slice | solution.py:14
  11.7 19.6 %copy-start = (bf16[8,64,2,512]{3,2,1,0:T(2,128)(2,1)S(1)}, bf16[8,64,2,512]{3,2,1,0:T(2,128)(2,1)}, u32[]{:S(2)}) copy-start(bf16[8,64,2,512]{3,2,1,0:T(2,128)(2,1)} %param.3) | copy-start | bytes 3145732
  11.7 384.6 %all-to-all-start = ((bf16[64,2,512,1,64]{2,4,1,3,0:T(8,128)(2,1)}), bf16[64,2,512,1,64]{2,4,1,3,0:T(8,128)(2,1)}, u32[]{:S(2)}, u32[]{:S(2)}) async-start(bf16[64,2,512,1,64]{2,4,1,3,0:T(8,128)(2,1)} %stack.2), calls=%async_computation | async-start | bytes 16777216 | tf_op jit(solution)/shard_map/all_to_all | solution.py:23
  30.8 681.8 %reduce-scatter.2.cloned.1.call-start = ((), (), s32[]{:S(2)}) async-start(), calls=%async_computation.3 | async-start | bytes 4718592 | tf_op jit(solution)/shard_map/reduce_scatter | solution.py:30
Sparse Core Ops, SparseCore 0:
  673.9 38.6 reduce-scatter.1

commit v2 on v0

--- a/solution.py
+++ b/solution.py
@@ -22,8 +22,14 @@
         lax.all_gather(cycle_integrals, "tr", axis=3, tiled=True),
         preferred_element_type=jnp.float32,
     )
-    moved_parts = lax.all_to_all(
-        partial_value.astype(jnp.bfloat16), "tr", split_axis=3, concat_axis=1, tiled=True
+    moved_parts = jnp.concatenate(
+        lax.all_to_all(
+            jnp.stack(jnp.split(partial_value.astype(jnp.bfloat16), lax.axis_size("tr"), axis=3)),
+            "tr",
+            0,
+            0,
+        ),
+        axis=1,
     )
     moved = lax.psum_scatter(
         moved_parts.astype(jnp.float32).astype(jnp.bfloat16), "ct", scatter_dimension=0, tiled=True

time: 503 us -> 511 us (1.016)
  local copies, waits for them, and re-layouts: 86.8 us -> 96.1 us
    reshape x0 -> x3, local copies, waits for them, and re-layouts: none -> 34.5 us  [per_device(): jnp.concatenate(lax.all_to_all(jnp.stack(jnp.split(partial_value.astype(j...]
    all_to_all x2 -> x0, local copies, waits for them, and re-layouts: 24 us -> none  [per_device(): lax.all_to_all(partial_value.astype(jnp.bfloat16), 'tr', split_axis=3, co...]
    convert_element_type x1 -> x0, local copies, waits for them, and re-layouts: 10 us -> none  [per_device(): partial_value.astype(jnp.bfloat16)]
    unnamed x3 -> x68, local copies, waits for them, and re-layouts: 30.6 us -> 39.4 us
where the time goes in v2:
time: 511 us; the launch traced here: 509 us
  waiting for transfers between devices  200 us (39%)
  blocking collectives  188 us (37%)
  local copies, waits for them, and re-layouts  96.1 us (19%)
  between operations  13.7 us (3%)
  matrix products  8.08 us (2%)
    all_to_all x1, blocking collectives, per_device(): lax.all_to_all(jnp.stack(jnp.split(partial_value.astype(jnp.bfloat16), la...  188 us
    all_gather x1, waiting for transfers between devices, per_device(): lax.all_gather(cycle_integrals, 'tr', axis=3, tiled=True)  158 us
    reduce_scatter x1, waiting for transfers between devices, per_device(): lax.psum_scatter(moved_parts.astype(jnp.float32).astype(jnp.bfloat16), 'c...  41.4 us
    unnamed x68, local copies, waits for them, and re-layouts  39.4 us
    reshape x3, local copies, waits for them, and re-layouts, per_device(): jnp.concatenate(lax.all_to_all(jnp.stack(jnp.split(partial_value.astype(j...  34.5 us
    all_gather x1, local copies, waits for them, and re-layouts, per_device(): lax.all_gather(cycle_integrals, 'tr', axis=3, tiled=True)  21.2 us
  transfers between devices with their start and end apart: 2, of which 2 were waited for; matrix products, arithmetic and copies ran while one was open for 1% of the time, Pallas kernels for 0%

profile of v2, /device:TPU:2, one launch (start us, length us, event | category | flops | bytes accessed | tf_op | source)
XLA Modules:
  0.0 508.9 jit_solution(9158225113865171625)
XLA Ops:
  6.5 1.7 copy.10
  8.3 0.7 slice.3
  9.0 0.9 fusion.8
  9.9 0.1 reshape.16
  10.1 2.3 multiply_multiply_fusion
  12.4 158.5 %all-gather.2.cloned.1.call-done = bf16[2,512,1,4096]{1,0,2,3:T(2,128)(2,1)} async-done(((bf16[2,512,1,64]{1,0,2,3:T(2,128)(2,1)}), bf16[2,512,1,4096]{1,0,2,3:T(2,128)(2,1)}) %all-gather.2.cloned.1.call-update) | async-done | bytes 8388624 | tf_op jit(solution)/shard_map/all_gather | solution.py:22
  170.8 21.2 %copy.11 = bf16[2,512,1,4096]{3,1,0,2:T(8,128)(2,1)} copy(bf16[2,512,1,4096]{1,0,2,3:T(2,128)(2,1)} %all-gather.2.cloned.1.call-done) | data formatting | bytes 16777216 | tf_op jit(solution)/shard_map/all_gather | solution.py:22
  192.0 8.1 %fusion.4 = bf16[8,64,1,4096]{3,1,0,2:T(8,128)(2,1)S(1)} fusion(bf16[2,512,1,4096]{3,1,0,2:T(8,128)(2,1)} %copy.11, bf16[8,64,2,512]{3,2,1,0:T(2,128)(2,1)S(1)} %multiply_multiply_fusion), kind=kOutput, calls=%fused_computation.3 | convolution fusion | flops 4297064448 | bytes 13631488 | tf_op jit(solution)/shard_map/iakc,kcjb->iajb/dot_general | solution.py:19
  200.1 0.1 constant_dynamic-update-slice_fusion.62
  200.3 0.1 constant_dynamic-update-slice_fusion.60
  200.5 0.1 constant_dynamic-update-slice_fusion.58
  200.7 0.1 constant_dynamic-update-slice_fusion.56
  200.9 0.1 constant_dynamic-update-slice_fusion.54
  201.1 0.1 constant_dynamic-update-slice_fusion.52
  201.3 0.1 constant_dynamic-update-slice_fusion.50
  201.5 0.1 constant_dynamic-update-slice_fusion.48
  201.6 0.1 constant_dynamic-update-slice_fusion.46
  201.8 0.1 constant_dynamic-update-slice_fusion.44
  202.0 0.1 constant_dynamic-update-slice_fusion.42
  202.2 0.1 constant_dynamic-update-slice_fusion.40
  202.4 0.1 constant_dynamic-update-slice_fusion.38
  202.6 0.1 constant_dynamic-update-slice_fusion.36
  202.8 0.1 constant_dynamic-update-slice_fusion.34
  203.0 0.1 constant_dynamic-update-slice_fusion.32
  203.2 0.1 constant_dynamic-update-slice_fusion.30
  203.3 0.1 constant_dynamic-update-slice_fusion.28
  203.5 0.1 constant_dynamic-update-slice_fusion.26
  203.7 0.1 constant_dynamic-update-slice_fusion.24
  203.9 0.1 constant_dynamic-update-slice_fusion.22
  204.1 0.1 constant_dynamic-update-slice_fusion.20
  204.3 0.1 constant_dynamic-update-slice_fusion.18
  204.5 0.1 constant_dynamic-update-slice_fusion.16
  204.7 0.1 constant_dynamic-update-slice_fusion.14
  204.8 0.1 constant_dynamic-update-slice_fusion.12
  205.0 0.1 constant_dynamic-update-slice_fusion.10
  205.2 0.1 constant_dynamic-update-slice_fusion.8
  205.4 0.1 constant_dynamic-update-slice_fusion.6
  205.6 0.1 constant_dynamic-update-slice_fusion.4
  205.8 0.1 constant_dynamic-update-slice_fusion.2
  206.0 0.1 constant_dynamic-update-slice_fusion
  206.1 3.2 copy-done
  209.3 14.3 %reshape.23 = bf16[64,2,16384]{2,1,0:T(2,128)(2,1)} reshape(bf16[64,1,8,64,64]{4,3,2,1,0:T(8,128)(2,1)} %bitcast.283) | data formatting | bytes 8388608
  223.6 187.9 %all_to_all.5 = bf16[64,2,16384]{2,1,0:T(2,128)(2,1)} all-to-all(bf16[64,2,16384]{2,1,0:T(2,128)(2,1)} %reshape.23), channel_id=1, replica_groups=mesh['tr'=64,'ct'=8] {'tr'}, dimensions={0} | all-to-all | bytes 8388608 | tf_op jit(solution)/shard_map/all_to_all | solution.py:26
  411.6 14.6 %reshape.24 = bf16[64,1,8,64,64]{4,3,2,1,0:T(8,128)(2,1)} reshape(bf16[64,2,16384]{2,1,0:T(2,128)(2,1)} %all_to_all.5) | data formatting | bytes 8388608
  426.2 10.3 %bitcast_bitcast_fusion = bf16[8,64,64,1,64]{4,2,0,3,1:T(8,128)(2,1)} fusion(bf16[64,1,8,64,64]{4,3,2,1,0:T(8,128)(2,1)} %reshape.24), kind=kLoop, calls=%fused_computation.137 | loop fusion | bytes 8388608 | tf_op jit(solution)/shard_map/reshape | solution.py:25
  436.5 12.1 %copy.13 = bf16[8,64,64,1,64]{2,1,4,0,3:T(8,128)(2,1)} copy(bf16[8,64,64,1,64]{4,2,0,3,1:T(8,128)(2,1)} %bitcast_bitcast_fusion) | data formatting | bytes 8388608 | tf_op jit(solution)/shard_map/reshape | solution.py:25
  448.6 12.0 %reshape.19 = bf16[8,4096,1,64]{1,3,0,2:T(8,128)(2,1)} reshape(bf16[8,64,64,1,64]{2,1,4,0,3:T(8,128)(2,1)} %copy.13) | data formatting | bytes 8388608 | tf_op jit(solution)/shard_map/reshape | solution.py:25
  460.7 41.4 %reduce-scatter.2.cloned.1.call-done = bf16[1,4096,1,64]{1,3,0,2:T(8,128)(2,1)} async-done(((bf16[8,4096,1,64]{1,3,0,2:T(8,128)(2,1)}), bf16[1,4096,1,64]{1,3,0,2:T(8,128)(2,1)}) %reduce-scatter.2.cloned.1.call-update) | async-done | bytes 524304 | tf_op jit(solution)/shard_map/reduce_scatter | solution.py:34
  (39 shorter events, 1.8 us)
Async XLA Ops:
  6.5 164.3 %all-gather.2.cloned.1.call-start = ((), (), s32[]{:S(2)}) async-start(), calls=%async_computation.2 | async-start | bytes 8519680 | tf_op jit(solution)/shard_map/all_gather | solution.py:22
  8.3 493.8 %reduce-scatter.2.cloned.1.call-start = ((), (), s32[]{:S(2)}) async-start(), calls=%async_computation.3 | async-start | bytes 4718592 | tf_op jit(solution)/shard_map/reduce_scatter | solution.py:34
  206.1 3.2 copy-start
Sparse Core Ops, SparseCore 0:
  10.3 160.4 all-gather.1
  460.8 41.2 reduce-scatter.1
